TPU v7x, 256 devices: a whole 4x4x8 slice. The times are simulated.
256 devices in a mesh: seq: 32 (over z_lo, x, core), cam: 4 (over y), tp: 2 (over z_hi).
Axes of the slice: x: 4, y: 4, z: 8 (z_hi: 2, z_lo: 4; z = z_hi * 4 + z_lo), core: 2. Of those that a mesh axis runs over, the one named last changes fastest.
Arguments:
- pixel_feature: bfloat16 [32768, 2048], P(('seq', 'cam'), 'tp'), may hold values from -6 to 6
- depth_score: float32 [32768, 59], P(('seq', 'cam')), may hold values from 0.05 to 5
- depth_bin: int32 [32768, 4], P(('seq', 'cam')), may hold values from 0 to 58
- cell_owner: int32 [131072, 1], P(('seq', 'cam')), may hold values from 0 to 31; in each aligned block of 1024 rows (0 to 1023, 1024 to 2047, ...) at most 64 rows name the same one
- cell_local: int32 [32768, 4], P(('seq', 'cam')), may hold values from 0 to 7
- frame_keep: int32 [64], replicated, may hold values 0 or 1
- norm_gain: float32 [2048], P('tp'), may hold values from 0.1 to 1.9
- w_query: bfloat16 [2048, 2048], P(None, ('cam', 'tp')), may hold values from -1.5 to 1.5
- w_key: bfloat16 [2048, 2048], P(None, ('cam', 'tp')), may hold values from -0.375 to 0.375
- w_value: bfloat16 [2048, 2048], P(None, ('cam', 'tp')), may hold values from -0.125 to 0.125
Outputs:
- attended: bfloat16 [16384, 2048], P('seq', ('cam', 'tp'))
Inputs may be any that keep to these rules, and one draw needn't show every extreme that they name: `cell_owner`: among the 1024 points of one index of seq and cam (aligned blocks of rows), no owner is named more than 64 times, a bound that some block reaches.
All inputs are finite; a program needn't handle non-finite values.
Results may differ from a plain program's by a relative error of at most 0.028.
The roundings to bfloat16 on the way count: a program that leaves them out, or rounds other values in their place, can miss the bound.
Values may be sent and summed in bfloat16 or wider, within the bound.
A program may use at most 64 MiB of HBM per device.

v0:
```python
import jax
import jax.numpy as jnp
from jax import lax
from jax.sharding import PartitionSpec as P

D = 2048
HD = 128
CELL_DEV = 8
epsilon = 1e-05
block_rows = 512


def attend(state, query, query_start, keys, values, key_start, frame_keep):
    frames = frame_keep.shape[0]
    frame_query = (query_start + jnp.arange(query.shape[0], dtype=jnp.int32)) % frames
    frame_key = (key_start + jnp.arange(keys.shape[0], dtype=jnp.int32)) % frames
    frame_list = jnp.arange(frames, dtype=jnp.int32)
    kept = jnp.sum(
        jnp.where(frame_key[:, None] == frame_list[None, :], frame_keep[None, :], 0), axis=1
    )
    allowed = (frame_key[None, :] <= frame_query[:, None]) & (
        (kept[None, :] > 0) | (frame_key[None, :] == frame_query[:, None])
    )
    scores = jnp.einsum("qhd,khd->hqk", query, keys, preferred_element_type=jnp.float32) * (
        1.0 / HD**0.5
    )
    accum, peak, total = state
    new_peak = jnp.maximum(peak, jnp.max(jnp.where(allowed[None], scores, -1e30), axis=2))
    factor = jnp.exp(peak - new_peak)
    expo = jnp.where(allowed[None], jnp.exp(scores - new_peak[:, :, None]), 0.0)
    mixed = jnp.einsum(
        "hqk,khd->hqd", expo.astype(jnp.bfloat16), values, preferred_element_type=jnp.float32
    )
    return (accum * factor[:, :, None] + mixed, new_peak, total * factor + jnp.sum(expo, axis=2))


def local(
    pixel_feature,
    depth_score,
    depth_bin,
    cell_owner,
    cell_local,
    frame_keep,
    norm_gain,
    w_query,
    w_key,
    w_value,
):
    pixels, half = pixel_feature.shape
    keep_count = depth_bin.shape[1]
    points = pixels * keep_count
    seq_count = lax.axis_size("seq")
    seq_index = lax.axis_index("seq")
    frames = frame_keep.shape[0]
    frames_dev = frames // seq_count
    tokens_dev = CELL_DEV * frames
    capacity = 2 * points // seq_count
    prob = depth_score / jnp.sum(depth_score, axis=1, keepdims=True)
    bins = jnp.arange(depth_score.shape[1], dtype=jnp.int32)
    picked = jnp.sum(
        jnp.where(depth_bin[:, :, None] == bins[None, None, :], prob[:, None, :], 0.0), axis=2
    )
    weight = picked.astype(jnp.bfloat16)
    point_index = jnp.arange(points, dtype=jnp.int32).reshape(pixels, keep_count)
    local_frame = point_index // (points // frames_dev)
    owner = cell_owner[:, 0].reshape(pixels, keep_count)
    owner_flat = owner.reshape(points)
    hits = (owner_flat[:, None] == jnp.arange(seq_count, dtype=jnp.int32)[None, :]).astype(
        jnp.int32
    )
    rank = jnp.sum(jnp.cumsum(hits, axis=0) * hits, axis=1) - 1
    slot = owner_flat * capacity + rank
    point_rows = jnp.repeat(pixel_feature, keep_count, axis=0)
    send_rows = jnp.zeros((seq_count * capacity, half), jnp.bfloat16).at[slot].set(point_rows)
    send_rows = send_rows.reshape(seq_count, capacity, half)
    frame_global = seq_index * frames_dev + local_frame
    describe = jnp.stack(
        [
            weight.reshape(points),
            cell_local.reshape(points).astype(jnp.bfloat16),
            frame_global.reshape(points).astype(jnp.bfloat16),
        ],
        axis=0,
    )
    send_meta = jnp.zeros((3, seq_count * capacity), jnp.bfloat16).at[:, slot].set(describe)
    send_meta = send_meta.reshape(3, seq_count, capacity).transpose(1, 0, 2)
    got_rows, got_meta = (
        lax.all_to_all(send_rows, "seq", split_axis=0, concat_axis=0, tiled=True),
        lax.all_to_all(send_meta, "seq", split_axis=0, concat_axis=0, tiled=True),
    )
    target = (
        got_meta[:, 1, :].astype(jnp.float32) * frames + got_meta[:, 2, :].astype(jnp.float32)
    ).reshape(-1)
    token_ids = jnp.arange(tokens_dev, dtype=jnp.float32)
    mixing = jnp.where(
        token_ids[:, None] == target[None, :], got_meta[:, 0, :].reshape(-1)[None, :], 0
    )
    pooled = jnp.dot(mixing, got_rows.reshape(-1, half), preferred_element_type=jnp.float32)
    bev = lax.psum(pooled, "cam")
    squares = lax.psum(jnp.sum(bev * bev, axis=1), "tp")
    normed = (bev * lax.rsqrt(squares[:, None] / D + epsilon) * norm_gain[None, :]).astype(
        jnp.bfloat16
    )
    width = w_query.shape[1]
    heads_dev = width // HD
    piece = lax.all_gather(normed, "tp", axis=1, tiled=True)
    query_sum = jnp.dot(piece, w_query, preferred_element_type=jnp.float32)
    key_sum = jnp.dot(piece, w_key, preferred_element_type=jnp.float32)
    value_sum = jnp.dot(piece, w_value, preferred_element_type=jnp.float32)
    query = query_sum.astype(jnp.bfloat16).reshape(tokens_dev, heads_dev, HD)
    keys = key_sum.astype(jnp.bfloat16).reshape(tokens_dev, heads_dev, HD)
    values = value_sum.astype(jnp.bfloat16).reshape(tokens_dev, heads_dev, HD)
    query_start = seq_index * tokens_dev
    start_state = (
        jnp.zeros((heads_dev, tokens_dev, HD), jnp.float32),
        jnp.full((heads_dev, tokens_dev), -1e30, jnp.float32),
        jnp.zeros((heads_dev, tokens_dev), jnp.float32),
    )
    piece_keys = lax.all_gather(keys, "seq", axis=0, tiled=True)
    piece_values = lax.all_gather(values, "seq", axis=0, tiled=True)
    count = piece_keys.shape[0]

    def one_block(index, inner):
        block_keys = lax.dynamic_slice_in_dim(piece_keys, index * block_rows, block_rows, 0)
        block_values = lax.dynamic_slice_in_dim(piece_values, index * block_rows, block_rows, 0)
        return attend(
            inner, query, query_start, block_keys, block_values, index * block_rows, frame_keep
        )

    accum, peak, total = lax.fori_loop(0, count // block_rows, one_block, start_state)
    result = accum / total[:, :, None]
    return result.transpose(1, 0, 2).reshape(tokens_dev, width).astype(jnp.bfloat16)


def solution(mesh):
    return jax.shard_map(
        local,
        mesh=mesh,
        in_specs=(
            P(("seq", "cam"), "tp"),
            P(("seq", "cam"), None),
            P(("seq", "cam"), None),
            P(("seq", "cam"), None),
            P(("seq", "cam"), None),
            P(),
            P("tp"),
            P(None, ("cam", "tp")),
            P(None, ("cam", "tp")),
            P(None, ("cam", "tp")),
        ),
        out_specs=P("seq", ("cam", "tp")),
        check_vma=False,
    )
```

profile of v0, /device:TPU:1, one launch (start us, length us, event | category | flops | bytes accessed | tf_op | source)
XLA Modules:
  0.0 587.0 jit_solution(16973022452448787255)
XLA Ops:
  11.1 9.0 %reduce-window.6 = s32[32,8,128]{2,1,0:T(8,128)S(1)} reduce-window(s32[32,8,128]{2,1,0:T(8,128)S(1)} %fusion.34, s32[]{:T(128)} %constant.143.clone.1), window={size=1x1x128 pad=0_0x0_0x127_0}, to_apply=%region_0.0 | reduce-window | flops 4161536 | bytes 262148 | tf_op jit(solution)/shard_map/reduce-window
  22.4 3.3 scatter_custom_fusion
  26.7 10.0 %all-to-all-start = ((bf16[32,3,64]{2,1,0:T(4,128)(2,1)}), bf16[32,3,64]{2,1,0:T(4,128)(2,1)S(1)}, u32[]{:S(2)}, u32[]{:S(2)}) async-start(bf16[32,3,64]{2,1,0:T(4,128)(2,1)} %bitcast.8), calls=%async_computation | async-start | bytes 65536 | tf_op jit(solution)/shard_map/all_to_all | solution.py:89
  38.4 2.1 reshape.333
  40.4 8.6 %scatter_custom_fusion.1 = bf16[2048,1024]{1,0:T(8,128)(2,1)} fusion(s32[1024]{0:T(1024)S(1)} %bitcast.76, bf16[1024,1024]{1,0:T(8,128)(2,1)} %reshape.333, bf16[]{:T(256)} %constant.146.clone.1), kind=kCustom, calls=%fused_computation.44 | custom fusion | bytes 4194816 | tf_op jit(solution)/shard_map/scatter | solution.py:74
  49.0 7.8 %all-to-all-start.1 = ((bf16[32,64,1024]{2,1,0:T(8,128)(2,1)}), bf16[32,64,1024]{2,1,0:T(8,128)(2,1)}, u32[]{:S(2)}, u32[]{:S(2)}) async-start(bf16[32,64,1024]{2,1,0:T(8,128)(2,1)} %bitcast.65), calls=%async_computation.1 | async-start | bytes 8388608 | tf_op jit(solution)/shard_map/all_to_all | solution.py:88
  57.2 92.7 %all-to-all-done.1 = bf16[32,64,1024]{2,1,0:T(8,128)(2,1)} async-done(((bf16[32,64,1024]{2,1,0:T(8,128)(2,1)}), bf16[32,64,1024]{2,1,0:T(8,128)(2,1)}, u32[]{:S(2)}, u32[]{:S(2)}) %all-to-all-start.1) | async-done | bytes 4194336 | tf_op jit(solution)/shard_map/all_to_all | solution.py:88
  149.9 5.9 fusion.22
  155.8 64.2 %all-reduce.2.cloned.1.call-done = f32[512,1024]{1,0:T(8,128)} async-done(((f32[512,1024]{1,0:T(8,128)}), f32[512,1024]{1,0:T(8,128)}) %all-reduce.2.cloned.1.call-update) | async-done | bytes 2097168 | tf_op jit(solution)/shard_map/psum | solution.py:99
  221.9 7.8 %psum.15 = f32[512]{0:T(512)S(1)} all-reduce(f32[512]{0:T(512)S(1)} %multiply_reduce_fusion), channel_id=1, replica_groups=mesh['seq'=32,'cam'=4,'tp'=2] {'tp'}, use_global_device_ids=true, to_apply=%region_9.10 | all-reduce | flops 512 | bytes 4096 | tf_op jit(solution)/shard_map/psum | solution.py:100
  231.2 65.9 %all-gather.4.cloned.1.call-done = bf16[512,2048]{1,0:T(8,128)(2,1)} async-done(((bf16[512,1024]{1,0:T(8,128)(2,1)}), bf16[512,2048]{1,0:T(8,128)(2,1)}) %all-gather.4.cloned.1.call-update) | async-done | bytes 2097168 | tf_op jit(solution)/shard_map/all_gather | solution.py:106
  297.2 2.5 convolution_convert_fusion
  300.6 2.0 convolution_convert_fusion.2
  303.5 2.6 convolution_convert_fusion.1
  306.3 59.7 %all-gather.8.cloned.1.call-done = bf16[16384,2,128]{2,0,1:T(8,128)(2,1)} async-done(((bf16[512,2,128]{2,0,1:T(8,128)(2,1)}), bf16[16384,2,128]{2,0,1:T(8,128)(2,1)}) %all-gather.8.cloned.1.call-update) | async-done | bytes 8388624 | tf_op jit(solution)/shard_map/all_gather | solution.py:120
  366.0 69.0 %all-gather.6.cloned.1.call-done = bf16[16384,2,128]{2,0,1:T(8,128)(2,1)} async-done(((bf16[512,2,128]{2,0,1:T(8,128)(2,1)}), bf16[16384,2,128]{2,0,1:T(8,128)(2,1)}) %all-gather.6.cloned.1.call-update) | async-done | bytes 8388624 | tf_op jit(solution)/shard_map/all_gather | solution.py:119
  435.0 144.5 %while.20 = (s32[]{:T(128)}, f32[2,512,128]{2,1,0:T(8,128)S(1)}, f32[2,512]{1,0:T(2,128)S(1)}, f32[2,512]{1,0:T(2,128)S(1)}, s32[]{:T(128)}, /*index=5*/s32[64]{...) while((s32[]{:T(128)}, f32[2,512,128]{2,1,0:T(8,128)S(1)}, ...), condition=%wide.region_14.15_spmd.clone, body=%wide.region_10.14_spmd.clone.sunk | while | flops 275760128 | bytes 9256399 | solution.py:130
  437.5 2.0 convolution_add_fusion.2
  442.0 2.0 convolution_add_fusion.2
  446.5 2.0 convolution_add_fusion.2
  451.0 2.0 convolution_add_fusion.2
  455.5 2.0 convolution_add_fusion.2
  460.1 2.0 convolution_add_fusion.2
  464.6 2.0 convolution_add_fusion.2
  469.1 2.0 convolution_add_fusion.2
  473.6 2.0 convolution_add_fusion.2
  482.7 2.0 convolution_add_fusion.2
  487.2 2.0 convolution_add_fusion.2
  491.7 2.0 convolution_add_fusion.2
  500.7 2.0 convolution_add_fusion.2
  505.2 2.0 convolution_add_fusion.2
  509.8 2.0 convolution_add_fusion.2
  (363 shorter events, 129.2 us)
Async XLA Ops:
  6.5 290.6 %copy-start = (bf16[2048,256]{1,0:T(8,128)(2,1)S(1)}, bf16[2048,256]{1,0:T(8,128)(2,1)}, u32[]{:S(2)}) copy-start(bf16[2048,256]{1,0:T(8,128)(2,1)} %param.21) | copy-start | bytes 3145732
  26.7 22.4 %all-to-all-start = ((bf16[32,3,64]{2,1,0:T(4,128)(2,1)}), bf16[32,3,64]{2,1,0:T(4,128)(2,1)S(1)}, u32[]{:S(2)}, u32[]{:S(2)}) async-start(bf16[32,3,64]{2,1,0:T(4,128)(2,1)} %bitcast.8), calls=%async_computation | async-start | bytes 65536 | tf_op jit(solution)/shard_map/all_to_all | solution.py:89
  49.0 100.9 %all-to-all-start.1 = ((bf16[32,64,1024]{2,1,0:T(8,128)(2,1)}), bf16[32,64,1024]{2,1,0:T(8,128)(2,1)}, u32[]{:S(2)}, u32[]{:S(2)}) async-start(bf16[32,64,1024]{2,1,0:T(8,128)(2,1)} %bitcast.65), calls=%async_computation.1 | async-start | bytes 8388608 | tf_op jit(solution)/shard_map/all_to_all | solution.py:88
  56.8 163.2 %all-reduce.2.cloned.1.call-start = ((), (), s32[]{:S(2)}) async-start(), calls=%async_computation.2 | async-start | bytes 4194304 | tf_op jit(solution)/shard_map/psum | solution.py:99
  155.7 74.0 %copy-start.3 = (f32[1024]{0:T(1024)S(1)}, f32[1024]{0:T(1024)}, u32[]{:S(2)}) copy-start(f32[1024]{0:T(1024)} %param.18) | copy-start | bytes 12292
  155.8 141.4 %all-gather.4.cloned.1.call-start = ((), (), s32[]{:S(2)}) async-start(), calls=%async_computation.3 | async-start | bytes 3145728 | tf_op jit(solution)/shard_map/all_gather | solution.py:106
  220.0 9.7 %copy-start.1 = (f32[512,1024]{1,0:T(8,128)S(1)}, f32[512,1024]{1,0:T(8,128)}, u32[]{:S(2)}) copy-start(f32[512,1024]{1,0:T(8,128)} %all-reduce.2.cloned.1.call-done) | copy-start | bytes 6291460
  231.0 135.0 %all-gather.8.cloned.1.call-start = ((), (), s32[]{:S(2)}) async-start(), calls=%async_computation.5 | async-start | bytes 8650752 | tf_op jit(solution)/shard_map/all_gather | solution.py:120
  297.2 3.4 copy-start.4
  300.5 134.4 %all-gather.6.cloned.1.call-start = ((), (), s32[]{:S(2)}) async-start(), calls=%async_computation.4 | async-start | bytes 8650752 | tf_op jit(solution)/shard_map/all_gather | solution.py:119
  303.5 131.5 %copy-start.2 = (s32[64]{0:T(128)S(1)}, s32[64]{0:T(128)}, u32[]{:S(2)}) copy-start(s32[64]{0:T(128)} %param.17) | copy-start | bytes 772
Sparse Core Ops, SparseCore 0:
  155.9 64.0 all-reduce.1
  231.1 66.0 all-gather.3
  300.7 65.2 all-gather.7
  367.7 67.1 all-gather.5
where the time goes:
time: 590 us; the launch traced here: 587 us
  waiting for transfers between devices  352 us (60%)
  matrix products  124 us (21%)
  other arithmetic  50.4 us (9%)
  local copies, waits for them, and re-layouts  19.9 us (3%)
  starting transfers between devices  18.1 us (3%)
  between operations  13.3 us (2%)
  blocking collectives  7.76 us (1%)
    all_to_all x1, waiting for transfers between devices, local(): lax.all_to_all(send_rows, 'seq', split_axis=0, concat_axis=0, tiled=True)  92.7 us
    all_gather x1, waiting for transfers between devices, local(): piece_keys = lax.all_gather(keys, 'seq', axis=0, tiled=True)  69 us
    all_gather x1, waiting for transfers between devices, local(): piece = lax.all_gather(normed, 'tp', axis=1, tiled=True)  65.9 us
    psum x1, waiting for transfers between devices, local(): bev = lax.psum(pooled, 'cam')  64.2 us
    dot_general x32, matrix products, attend(): jnp.einsum('hqk,khd->hqd', expo.astype(jnp.bfloat16), values, preferred_e...  62.6 us
    all_gather x1, waiting for transfers between devices, local(): piece_values = lax.all_gather(values, 'seq', axis=0, tiled=True)  59.7 us
    dot_general x32, matrix products, attend(): jnp.einsum('qhd,khd->hqk', query, keys, preferred_element_type=jnp.float32)  48.2 us
    reduce_sum x32, other arithmetic, attend(): jnp.sum(expo, axis=2)  15.9 us
  transfers between devices with their start and end apart: 6, of which 5 were waited for; matrix products, arithmetic and copies ran while one was open for 3% of the time, Pallas kernels for 0%

commit v1 on v0

--- a/solution.py
+++ b/solution.py
@@ -117,7 +117,9 @@
         jnp.zeros((heads_dev, tokens_dev), jnp.float32),
     )
     piece_keys = lax.all_gather(keys, "seq", axis=0, tiled=True)
-    piece_values = lax.all_gather(values, "seq", axis=0, tiled=True)
+    piece_values = jnp.concatenate(
+        lax.all_to_all(jnp.stack([values] * lax.axis_size("seq")), "seq", 0, 0), axis=0
+    )
     count = piece_keys.shape[0]
 
     def one_block(index, inner):

time: 590 us -> 745 us (1.26)
  waiting for transfers between devices: 352 us -> 443 us
  local copies, waits for them, and re-layouts: 19.9 us -> 75.6 us
    all_to_all x0 -> x1, waiting for transfers between devices: none -> 220 us  [local(): lax.all_to_all(jnp.stack([values] * lax.axis_size('seq')), 'seq', 0, 0)]
    all_gather x1, waiting for transfers between devices: 69 us -> 0.01 us  [local(): piece_keys = lax.all_gather(keys, 'seq', axis=0, tiled=True)]
    all_gather x1 -> x0, waiting for transfers between devices: 59.7 us -> none  [local(): piece_values = lax.all_gather(values, 'seq', axis=0, tiled=True)]
    while x32 -> x160, local copies, waits for them, and re-layouts: 0.08 us -> 42.9 us
    all_to_all x0 -> x1, local copies, waits for them, and re-layouts: none -> 7.59 us  [local(): lax.all_to_all(jnp.stack([values] * lax.axis_size('seq')), 'seq', 0, 0)]
  transfers between devices with their start and end apart: 6 -> 6, of which waited for: 5 -> 4; matrix products, arithmetic and copies ran while one was open for 3% -> 3% of each run, Pallas kernels for 0% -> 0%
where the time goes in v1:
time: 745 us; the launch traced here: 741 us
  waiting for transfers between devices  443 us (59%)
  matrix products  124 us (17%)
  local copies, waits for them, and re-layouts  75.6 us (10%)
  other arithmetic  51.3 us (7%)
  starting transfers between devices  23.4 us (3%)
  between operations  13.3 us (2%)
  blocking collectives  7.94 us (1%)
    all_to_all x1, waiting for transfers between devices, local(): lax.all_to_all(jnp.stack([values] * lax.axis_size('seq')), 'seq', 0, 0)  220 us
    all_to_all x1, waiting for transfers between devices, local(): lax.all_to_all(send_rows, 'seq', split_axis=0, concat_axis=0, tiled=True)  92.7 us
    all_gather x1, waiting for transfers between devices, local(): piece = lax.all_gather(normed, 'tp', axis=1, tiled=True)  66.2 us
    psum x1, waiting for transfers between devices, local(): bev = lax.psum(pooled, 'cam')  64.2 us
    dot_general x32, matrix products, attend(): jnp.einsum('hqk,khd->hqd', expo.astype(jnp.bfloat16), values, preferred_e...  61.4 us
    dot_general x32, matrix products, attend(): jnp.einsum('qhd,khd->hqk', query, keys, preferred_element_type=jnp.float32)  50.7 us
    while x160, local copies, waits for them, and re-layouts  42.9 us
    reduce_sum x32, other arithmetic, attend(): jnp.sum(expo, axis=2)  15.9 us
  transfers between devices with their start and end apart: 6, of which 4 were waited for; matrix products, arithmetic and copies ran while one was open for 3% of the time, Pallas kernels for 0%

profile of v1, /device:TPU:1, one launch (start us, length us, event | category | flops | bytes accessed | tf_op | source)
XLA Modules:
  0.0 741.0 jit_solution(11963761777214676723)
XLA Ops:
  7.3 9.0 %reduce-window.6 = s32[32,8,128]{2,1,0:T(8,128)S(1)} reduce-window(s32[32,8,128]{2,1,0:T(8,128)S(1)} %fusion.34, s32[]{:T(128)} %constant.143.clone.1), window={size=1x1x128 pad=0_0x0_0x127_0}, to_apply=%region_0.0 | reduce-window | flops 4161536 | bytes 262148 | tf_op jit(solution)/shard_map/reduce-window
  22.4 3.3 scatter_custom_fusion
  26.6 10.0 %all-to-all-start = ((bf16[32,3,64]{2,1,0:T(4,128)(2,1)}), bf16[32,3,64]{2,1,0:T(4,128)(2,1)S(1)}, u32[]{:S(2)}, u32[]{:S(2)}) async-start(bf16[32,3,64]{2,1,0:T(4,128)(2,1)} %bitcast.8), calls=%async_computation | async-start | bytes 65536 | tf_op jit(solution)/shard_map/all_to_all | solution.py:89
  38.4 2.1 reshape.335
  40.4 8.6 %scatter_custom_fusion.1 = bf16[2048,1024]{1,0:T(8,128)(2,1)} fusion(s32[1024]{0:T(1024)S(1)} %bitcast.76, bf16[1024,1024]{1,0:T(8,128)(2,1)} %reshape.335, bf16[]{:T(256)} %constant.146.clone.1), kind=kCustom, calls=%fused_computation.44 | custom fusion | bytes 4194816 | tf_op jit(solution)/shard_map/scatter | solution.py:74
  49.0 7.8 %all-to-all-start.1 = ((bf16[32,64,1024]{2,1,0:T(8,128)(2,1)}), bf16[32,64,1024]{2,1,0:T(8,128)(2,1)}, u32[]{:S(2)}, u32[]{:S(2)}) async-start(bf16[32,64,1024]{2,1,0:T(8,128)(2,1)} %bitcast.64), calls=%async_computation.1 | async-start | bytes 8388608 | tf_op jit(solution)/shard_map/all_to_all | solution.py:88
  57.2 92.7 %all-to-all-done.1 = bf16[32,64,1024]{2,1,0:T(8,128)(2,1)} async-done(((bf16[32,64,1024]{2,1,0:T(8,128)(2,1)}), bf16[32,64,1024]{2,1,0:T(8,128)(2,1)}, u32[]{:S(2)}, u32[]{:S(2)}) %all-to-all-start.1) | async-done | bytes 4194336 | tf_op jit(solution)/shard_map/all_to_all | solution.py:88
  149.9 5.9 fusion.22
  155.8 64.2 %all-reduce.2.cloned.1.call-done = f32[512,1024]{1,0:T(8,128)} async-done(((f32[512,1024]{1,0:T(8,128)}), f32[512,1024]{1,0:T(8,128)}) %all-reduce.2.cloned.1.call-update) | async-done | bytes 2097168 | tf_op jit(solution)/shard_map/psum | solution.py:99
  220.0 2.0 multiply_reduce_fusion
  221.9 7.9 %psum.15 = f32[512]{0:T(512)S(1)} all-reduce(f32[512]{0:T(512)S(1)} %multiply_reduce_fusion), channel_id=1, replica_groups=mesh['seq'=32,'cam'=4,'tp'=2] {'tp'}, use_global_device_ids=true, to_apply=%region_9.10 | all-reduce | flops 512 | bytes 4096 | tf_op jit(solution)/shard_map/psum | solution.py:100
  231.2 66.2 %all-gather.3.cloned.1.call-done = bf16[512,2048]{1,0:T(8,128)(2,1)} async-done(((bf16[512,1024]{1,0:T(8,128)(2,1)}), bf16[512,2048]{1,0:T(8,128)(2,1)}) %all-gather.3.cloned.1.call-update) | async-done | bytes 2097168 | tf_op jit(solution)/shard_map/all_gather | solution.py:106
  297.3 2.3 convolution_convert_fusion
  299.9 5.2 stack.9
  305.1 5.5 all-to-all-start.2
  310.7 2.0 convolution_convert_fusion.2
  313.6 2.0 convolution_convert_fusion.1
  316.4 220.1 %all-to-all-done.2 = bf16[32,512,2,128]{3,1,2,0:T(8,128)(2,1)} async-done(((bf16[32,512,2,128]{3,1,2,0:T(8,128)(2,1)}), bf16[32,512,2,128]{3,1,2,0:T(8,128)(2,1)}, u32[]{:S(2)}, u32[]{:S(2)}) %all-to-all-start.2) | async-done | bytes 8388640 | tf_op jit(solution)/shard_map/all_to_all | solution.py:121
  536.5 7.6 %copy.64 = bf16[32,512,2,128]{3,1,0,2:T(8,128)(2,1)} copy(bf16[32,512,2,128]{3,1,2,0:T(8,128)(2,1)} %all-to-all-done.2) | data formatting | bytes 16777216 | tf_op jit(solution)/shard_map/all_to_all | solution.py:121
  544.1 188.5 %while.20 = (s32[]{:T(128)}, f32[2,512,128]{2,1,0:T(8,128)}, f32[2,512]{1,0:T(2,128)S(1)}, f32[2,512]{1,0:T(2,128)S(1)}, s32[]{:T(128)}, /*index=5*/s32[64]{0:T(...) while((s32[]{:T(128)}, f32[2,512,128]{2,1,0:T(8,128)}, ...), condition=%wide.region_14.15_spmd.clone, body=%wide.region_10.14_spmd.clone.sunk | while | flops 275760128 | bytes 13450751 | solution.py:132
  570.8 1.9 convolution_add_fusion.2
  576.6 1.9 convolution_add_fusion.2
  582.5 1.9 convolution_add_fusion.2
  594.3 1.9 convolution_add_fusion.2
  612.0 1.9 convolution_add_fusion.2
  629.6 1.9 convolution_add_fusion.2
  647.3 1.9 convolution_add_fusion.2
  665.0 1.9 convolution_add_fusion.2
  682.6 1.9 convolution_add_fusion.2
  700.3 1.9 convolution_add_fusion.2
  718.0 1.9 convolution_add_fusion.2
  732.5 2.0 copy_bitcast_fusion
  (492 shorter events, 178.3 us)
Async XLA Ops:
  6.5 290.8 %copy-start = (bf16[2048,256]{1,0:T(8,128)(2,1)S(1)}, bf16[2048,256]{1,0:T(8,128)(2,1)}, u32[]{:S(2)}) copy-start(bf16[2048,256]{1,0:T(8,128)(2,1)} %param.21) | copy-start | bytes 3145732
  26.6 22.4 %all-to-all-start = ((bf16[32,3,64]{2,1,0:T(4,128)(2,1)}), bf16[32,3,64]{2,1,0:T(4,128)(2,1)S(1)}, u32[]{:S(2)}, u32[]{:S(2)}) async-start(bf16[32,3,64]{2,1,0:T(4,128)(2,1)} %bitcast.8), calls=%async_computation | async-start | bytes 65536 | tf_op jit(solution)/shard_map/all_to_all | solution.py:89
  49.0 100.9 %all-to-all-start.1 = ((bf16[32,64,1024]{2,1,0:T(8,128)(2,1)}), bf16[32,64,1024]{2,1,0:T(8,128)(2,1)}, u32[]{:S(2)}, u32[]{:S(2)}) async-start(bf16[32,64,1024]{2,1,0:T(8,128)(2,1)} %bitcast.64), calls=%async_computation.1 | async-start | bytes 8388608 | tf_op jit(solution)/shard_map/all_to_all | solution.py:88
  56.8 163.2 %all-reduce.2.cloned.1.call-start = ((), (), s32[]{:S(2)}) async-start(), calls=%async_computation.3 | async-start | bytes 4194304 | tf_op jit(solution)/shard_map/psum | solution.py:99
  155.7 74.2 %copy-start.5 = (f32[1024]{0:T(1024)S(1)}, f32[1024]{0:T(1024)}, u32[]{:S(2)}) copy-start(f32[1024]{0:T(1024)} %param.18) | copy-start | bytes 12292
  155.8 141.6 %all-gather.3.cloned.1.call-start = ((), (), s32[]{:S(2)}) async-start(), calls=%async_computation.4 | async-start | bytes 3145728 | tf_op jit(solution)/shard_map/all_gather | solution.py:106
  220.0 9.9 %copy-start.1 = (f32[512,1024]{1,0:T(8,128)S(1)}, f32[512,1024]{1,0:T(8,128)}, u32[]{:S(2)}) copy-start(f32[512,1024]{1,0:T(8,128)} %all-reduce.2.cloned.1.call-done) | copy-start | bytes 6291460
  305.1 5.6 copy-start.6
  305.1 231.4 %all-to-all-start.2 = ((bf16[32,512,2,128]{3,1,2,0:T(8,128)(2,1)}), bf16[32,512,2,128]{3,1,2,0:T(8,128)(2,1)}, u32[]{:S(2)}, u32[]{:S(2)}) async-start(bf16[32,512,2,128]{3,1,2,0:T(8,128)(2,1)} %stack.9), calls=%async_computation.2 | async-start | bytes 16777216 | tf_op jit(solution)/shard_map/all_to_all | solution.py:121
  310.6 233.4 %all-gather.5.cloned.1.call-start = ((), (), s32[]{:S(2)}) async-start(), calls=%async_computation.5 | async-start | bytes 8650752 | tf_op jit(solution)/shard_map/all_gather | solution.py:119
  316.4 227.7 %copy-start.4 = (s32[64]{0:T(128)S(1)}, s32[64]{0:T(128)}, u32[]{:S(2)}) copy-start(s32[64]{0:T(128)} %param.17) | copy-start | bytes 772
  546.2 1.0 copy-start.2
  552.0 1.0 copy-start.2
  557.9 1.0 copy-start.2
  563.8 1.0 copy-start.2
  569.7 1.0 copy-start.2
  581.5 1.0 copy-start.2
  593.3 1.0 copy-start.2
  599.2 1.0 copy-start.2
  605.0 1.0 copy-start.2
  628.6 1.0 copy-start.2
  634.5 1.0 copy-start.2
  640.4 1.0 copy-start.2
  646.3 1.0 copy-start.2
  658.0 1.0 copy-start.2
  669.8 1.0 copy-start.2
  681.6 1.0 copy-start.2
  693.4 1.0 copy-start.2
  705.2 1.0 copy-start.2
  716.9 1.0 copy-start.2
  722.8 1.0 copy-start.2
  728.7 1.0 copy-start.2
  (43 other events, 38.6 us)
Sparse Core Ops, SparseCore 0:
  155.9 64.0 all-reduce.1
  231.3 66.0 all-gather.2
  313.7 184.5 all-gather.4
